TPU v7x, 32 devices: a whole 2x2x4 slice. The times are simulated.
32 devices in a mesh: wide: 16 (over z, y, x), narrow: 2 (over core).
Axes of the slice: x: 2, y: 2, z: 4, core: 2. Of those that a mesh axis runs over, the one named last changes fastest.
Arguments:
- pool_tokens: bfloat16 [12288, 2048], P(('wide', 'narrow')), may hold values from -6 to 6
- cotangent: bfloat16 [24576, 2048], P(('wide', 'narrow')), may hold values from -6 to 6
- slot_weights: bfloat16 [32, 3, 2048, 512], P(('wide', 'narrow')), may hold values from -6 to 6
- row_index: int32 [32, 768], P(('wide', 'narrow')), may hold values from 0 to 383
- route_weight: float32 [32, 768], P(('wide', 'narrow')), may hold values from 0.05 to 1
- slot_expert: int32 [32, 1], replicated, may hold values from 0 to 7
- next_expert: int32 [32, 1], replicated, may hold values from 0 to 7
- master: float32 [8, 3, 2048, 512], P(None, None, ('wide', 'narrow')), may hold values from -6 to 6
- moment_m: float32 [8, 3, 2048, 512], P(None, None, ('wide', 'narrow')), may hold values from -4 to 4
- moment_v: float32 [8, 3, 2048, 512], P(None, None, ('wide', 'narrow')), may hold values from 0.05 to 1
Outputs:
- token_grads: bfloat16 [12288, 2048], P(('wide', 'narrow'))
- master_next: float32 [8, 3, 2048, 512], P(None, None, ('wide', 'narrow'))
- moment_m_next: float32 [8, 3, 2048, 512], P(None, None, ('wide', 'narrow'))
- moment_v_next: float32 [8, 3, 2048, 512], P(None, None, ('wide', 'narrow'))
- next_weights: bfloat16 [32, 3, 2048, 512], P(('wide', 'narrow'))
Inputs may be any that keep to these rules, and one draw needn't show every extreme that they name: `slot_expert`: every one of the 8 experts is held by at least one slot; counts are uneven. `next_expert`: every one of the 8 experts is held by at least one slot; counts are uneven. `row_index`: indices into the pool of the slot's own device; a token may appear more than once.
All inputs are finite; a program needn't handle non-finite values.
Results may differ from a plain program's by a relative error of at most 0.0065.
Values may be sent and summed in bfloat16 or wider, within the bound.
A program may use at most 128 MiB of HBM per device.

v0:
```python
import jax
import jax.numpy as jnp
from jax import lax
from jax.sharding import PartitionSpec as P

EXPERTS = 8


def inner(left, right):
    return lax.dot_general(
        left, right, (((0,), (0,)), ((), ())), preferred_element_type=jnp.float32
    )


def against(left, right):
    return lax.dot_general(
        left, right, (((1,), (1,)), ((), ())), preferred_element_type=jnp.float32
    )


def slot_pass(rows, cotangent, weights, route):
    scale_in = weights.shape[1] ** (-0.5)
    scale_out = weights.shape[2] ** (-0.5)
    gate = jnp.dot(rows, weights[0], preferred_element_type=jnp.float32) * scale_in
    upper = jnp.dot(rows, weights[1], preferred_element_type=jnp.float32) * scale_in
    sigma = jax.nn.sigmoid(gate)
    active = gate * sigma
    hidden = (active * upper).astype(jnp.bfloat16)
    scaled = (route[:, None] * cotangent.astype(jnp.float32)).astype(jnp.bfloat16)
    back = jnp.dot(scaled, weights[2], preferred_element_type=jnp.float32) * scale_out
    d_gate = (back * upper * sigma * (1.0 + gate * (1.0 - sigma))).astype(jnp.bfloat16)
    d_up = (back * active).astype(jnp.bfloat16)
    grads = jnp.stack(
        [
            inner(rows, d_gate) * scale_in,
            inner(rows, d_up) * scale_in,
            inner(scaled, hidden) * scale_out,
        ]
    )
    inputs = (against(d_gate, weights[0]) + against(d_up, weights[1])) * scale_in
    return (grads, inputs)


def adam_step(grad, master, moment_m, moment_v):
    first = 0.9 * moment_m + 0.1 * grad
    second = 0.95 * moment_v + 0.05 * grad * grad
    fresh = master - 0.05 * (first / (jnp.sqrt(second) + 1e-08) + 0.1 * master)
    return (fresh, first, second)


def local(
    pool_tokens,
    cotangent,
    slot_weights,
    row_index,
    route_weight,
    slot_expert,
    next_expert,
    master,
    moment_m,
    moment_v,
):
    picked = row_index[0]
    rows = jnp.take(pool_tokens, picked, axis=0)
    grads, inputs = slot_pass(rows, cotangent, slot_weights[0], route_weight[0])
    token_grads = (
        jnp.zeros(pool_tokens.shape, jnp.float32).at[picked].add(inputs).astype(jnp.bfloat16)
    )
    wide_count = lax.axis_size("wide")
    narrow_count = lax.axis_size("narrow")
    members = wide_count * narrow_count
    parts, width, hidden_units = grads.shape
    block = width // members
    received = lax.all_to_all(grads, ("wide", "narrow"), split_axis=1, concat_axis=0, tiled=True)
    received = received.reshape(members, parts, block, hidden_units)
    owners = (slot_expert[:, 0][None, :] == jnp.arange(EXPERTS, dtype=jnp.int32)[:, None]).astype(
        jnp.float32
    )
    summed = jnp.einsum("es,skrh->ekrh", owners, received, precision=lax.Precision.HIGHEST)
    fresh, first, second = adam_step(summed, master, moment_m, moment_v)
    reordered = jnp.transpose(fresh.astype(jnp.bfloat16), (1, 0, 2, 3))
    outgoing = jnp.take(reordered, next_expert[:, 0], axis=1)
    arrived = lax.all_to_all(outgoing, ("wide", "narrow"), split_axis=1, concat_axis=2, tiled=True)
    next_weights = arrived.reshape(1, parts, width, hidden_units)
    return (token_grads, fresh, first, second, next_weights)


def solution(mesh):
    in_specs = (
        P(("wide", "narrow"), None),
        P(("wide", "narrow"), None),
        P(("wide", "narrow"), None, None, None),
        P(("wide", "narrow"), None),
        P(("wide", "narrow"), None),
        P(),
        P(),
        P(None, None, ("wide", "narrow"), None),
        P(None, None, ("wide", "narrow"), None),
        P(None, None, ("wide", "narrow"), None),
    )
    out_specs = (
        P(("wide", "narrow"), None),
        P(None, None, ("wide", "narrow"), None),
        P(None, None, ("wide", "narrow"), None),
        P(None, None, ("wide", "narrow"), None),
        P(("wide", "narrow"), None, None, None),
    )
    return jax.shard_map(local, mesh=mesh, in_specs=in_specs, out_specs=out_specs, check_vma=False)
```

profile of v0, /device:TPU:0, one launch (start us, length us, event | category | flops | bytes accessed | tf_op | source)
XLA Modules:
  0.0 623.7 jit_solution(776716893748135336)
XLA Ops:
  0.6 0.0 copy-start
  0.6 0.8 fusion.38
  1.5 0.7 reduce.2
  2.2 0.0 copy-done
  2.2 4.2 gather_fusion
  6.4 0.0 copy-start.5
  6.4 5.7 fusion.32
  12.1 0.0 copy-done.5
  12.1 0.0 copy-start.7
  12.1 4.6 fusion.29
  16.7 0.0 copy-done.7
  16.7 0.0 copy-start.9
  16.7 0.0 copy-start.11
  16.8 0.0 copy-start.12
  16.8 5.9 multiply_convert_fusion.2
  22.7 0.0 copy-done.9
  22.7 0.0 copy-done.11
  22.7 0.0 copy-done.12
  22.7 0.0 copy-start.6
  22.7 2.2 multiply_bitcast_fusion
  24.9 0.0 copy-done.6
  24.9 2.0 multiply_bitcast_fusion.1
  26.9 2.0 multiply_bitcast_fusion.2
  28.9 1.9 pad_maximum_fusion
  30.8 25.7 %copy.44 = f32[3,2048,512]{2,0,1:T(4,128)} copy(f32[3,2048,512]{2,1,0:T(8,128)S(1)} %pad_maximum_fusion) | data formatting | bytes 25165824 | tf_op jit(solution)/shard_map/stack | solution.py:33
  56.5 0.0 copy-start.10
  56.5 0.0 copy-start.8
  56.5 7.5 %all-to-all-start = ((f32[3,2048,512]{2,0,1:T(4,128)}), f32[3,2048,512]{2,0,1:T(4,128)}, u32[]{:S(2)}, u32[]{:S(2)}) async-start(f32[3,2048,512]{2,0,1:T(4,128)} %copy.44), calls=%async_computation | async-start | bytes 33554432 | tf_op jit(solution)/shard_map/all_to_all | solution.py:74
  64.0 0.0 copy-done.10
  64.0 372.5 %all-to-all-done = f32[3,2048,512]{2,0,1:T(4,128)} async-done(((f32[3,2048,512]{2,0,1:T(4,128)}), f32[3,2048,512]{2,0,1:T(4,128)}, u32[]{:S(2)}, u32[]{:S(2)}) %all-to-all-start) | async-done | bytes 12582944 | tf_op jit(solution)/shard_map/all_to_all | solution.py:74
  436.6 0.0 copy-done.8
  436.6 26.7 %convert_bitcast_fusion = (bf16[3,8,64,512]{3,1,2,0:T(8,128)(2,1)S(1)}, f32[8,3,64,512]{3,0,2,1:T(8,128)}, f32[8,3,64,512]{3,0,2,1:T(8,128)}, f32[8,3,64,512]{3,0,2,1:T(8,128)}) fusion(f32[8,3,64,512]{3,2,1,0:T(8,128)} %param.17, f32[8,3,64,512]{3,2,1,0:T(8,128)} %param.19, f32[8,3,64,512]{3,2,1,0:T(8,128)} %param.18, f32[3,32,64,512]{3,0,2,1:T(4,128)} %bitcast.10, ...), kind=kOutput, calls=%fused_computation.38 | convolution fusion | flops 313000192 | bytes 33030272 | tf_op jit(solution)/shard_map/es,skrh->ekrh/dot_general | solution.py:79
  463.2 0.5 copy.50
  463.8 3.7 gather_fusion.1
  467.4 6.1 select_bitcast_fusion
  473.5 3.8 all-to-all-start.1
  477.3 6.1 fusion.9
  483.4 6.0 fusion.13
  489.4 18.8 %scatter_custom_fusion = f32[384,2048]{1,0:T(8,128)} fusion(s32[768]{0:T(1024)S(1)} %fusion.38, f32[768,2048]{1,0:T(8,128)} %fusion.9, f32[768,2048]{1,0:T(8,128)} %fusion.13, f32[]{:T(128)} %constant.13.clone.1, f32[]{:T(128)} %constant.15.clone.1), kind=kCustom, calls=%fused_computation.8 | custom fusion | flops 4718592 | bytes 15728648 | tf_op jit(solution)/shard_map/scatter-add | solution.py:67
  508.2 0.0 copy-start.4
  508.2 3.4 convert_element_type.26
  511.6 0.0 copy-done.4
  511.6 0.0 copy-start.3
  511.6 3.5 copy.52
  515.1 0.0 copy-done.3
  515.1 0.0 copy-start.2
  515.1 3.5 copy.53
  518.6 0.0 copy-done.2
  518.6 3.5 copy.54
  522.1 94.9 %all-to-all-done.1 = bf16[3,32,64,512]{3,2,0,1:T(8,128)(2,1)} async-done(((bf16[3,32,64,512]{3,2,0,1:T(8,128)(2,1)}), bf16[3,32,64,512]{3,2,0,1:T(8,128)(2,1)}, u32[]{:S(2)}, u32[]{:S(2)}) %all-to-all-start.1) | async-done | bytes 6291488 | tf_op jit(solution)/shard_map/all_to_all | solution.py:83
  617.0 0.0 copy-start.1
  617.0 6.4 %copy.51 = bf16[3,32,64,512]{3,2,1,0:T(8,128)(2,1)} copy(bf16[3,32,64,512]{3,2,0,1:T(8,128)(2,1)} %all-to-all-done.1) | data formatting | bytes 12582912 | tf_op jit(solution)/shard_map/all_to_all | solution.py:83
  623.5 0.0 copy-done.1
  (6 shorter events, 0.0 us)
Async XLA Ops:
  0.6 1.6 copy-start
  6.4 5.7 copy-start.5
  12.1 4.6 copy-start.7
  16.7 6.0 copy-start.9
  16.7 6.0 copy-start.11
  16.8 6.0 copy-start.12
  22.7 2.2 copy-start.6
  56.5 7.5 %copy-start.10 = (s32[32,1]{0,1:T(1,128)S(1)}, s32[32,1]{0,1:T(1,128)}, u32[]{:S(2)}) copy-start(s32[32,1]{0,1:T(1,128)} %param.16) | copy-start | bytes 388
  56.5 380.1 %copy-start.8 = (s32[32,1]{0,1:T(1,128)S(1)}, s32[32,1]{0,1:T(1,128)}, u32[]{:S(2)}) copy-start(s32[32,1]{0,1:T(1,128)} %param.15) | copy-start | bytes 388
  56.5 380.1 %all-to-all-start = ((f32[3,2048,512]{2,0,1:T(4,128)}), f32[3,2048,512]{2,0,1:T(4,128)}, u32[]{:S(2)}, u32[]{:S(2)}) async-start(f32[3,2048,512]{2,0,1:T(4,128)} %copy.44), calls=%async_computation | async-start | bytes 33554432 | tf_op jit(solution)/shard_map/all_to_all | solution.py:74
  473.5 143.5 %all-to-all-start.1 = ((bf16[3,32,64,512]{3,2,0,1:T(8,128)(2,1)}), bf16[3,32,64,512]{3,2,0,1:T(8,128)(2,1)}, u32[]{:S(2)}, u32[]{:S(2)}) async-start(bf16[3,32,64,512]{3,2,0,1:T(8,128)(2,1)} %select_bitcast_fusion), calls=%async_computation.1 | async-start | bytes 12582912 | tf_op jit(solution)/shard_map/all_to_all | solution.py:83
  508.2 3.4 copy-start.4
  511.6 3.5 copy-start.3
  515.1 3.5 copy-start.2
  617.0 6.4 %copy-start.1 = (bf16[384,2048]{1,0:T(8,128)(2,1)S(1)}, bf16[384,2048]{1,0:T(8,128)(2,1)}, u32[]{:S(2)}) copy-start(bf16[384,2048]{1,0:T(8,128)(2,1)} %param.10) | copy-start | bytes 4718596
where the time goes:
time: 632 us; the launch traced here: 624 us
  waiting for transfers between devices  467 us (74%)
  matrix products  61.1 us (10%)
  local copies, waits for them, and re-layouts  51.1 us (8%)
  other arithmetic  31.7 us (5%)
  starting transfers between devices  11.2 us (2%)
    all_to_all x1, waiting for transfers between devices, local(): lax.all_to_all(grads, ('wide', 'narrow'), split_axis=1, concat_axis=0, ti...  373 us
    all_to_all x1, waiting for transfers between devices, local(): lax.all_to_all(outgoing, ('wide', 'narrow'), split_axis=1, concat_axis=2,...  94.9 us
    dot_general x1, matrix products, local(): jnp.einsum('es,skrh->ekrh', owners, received, precision=lax.Precision.HIG...  26.7 us
    another operation x1, local copies, waits for them, and re-layouts, slot_pass(): jnp.stack([inner(rows, d_gate) * scale_in, inner(rows, d_up) * scale_in,...  25.7 us
    scatter-add x1, other arithmetic, local(): jnp.zeros(pool_tokens.shape, jnp.float32).at[picked].add(inputs)  18.8 us
  transfers between devices with their start and end apart: 2, of which 2 were waited for; matrix products, arithmetic and copies ran while one was open for 7% of the time, Pallas kernels for 0%

commit v1 on v0

v1 whole, which is shorter than its diff:
```python
import functools

import jax
import jax.numpy as jnp
from jax import lax
from jax.experimental import pallas as pl
from jax.experimental.pallas import tpu as pltpu
from jax.sharding import PartitionSpec as P

EXPERTS = 8
MESH = pl.DeviceIdType.MESH
ROW_TILE = 16
COL_TILE = 256
UNROLL = 4


def inner(left, right):
    return lax.dot_general(
        left, right, (((0,), (0,)), ((), ())), preferred_element_type=jnp.float32
    )


def against(left, right):
    return lax.dot_general(
        left, right, (((1,), (1,)), ((), ())), preferred_element_type=jnp.float32
    )


def slot_pass(pool, picked, cotangent, weights, route):
    scale_in = weights.shape[1] ** (-0.5)
    scale_out = weights.shape[2] ** (-0.5)
    tokens = jnp.arange(pool.shape[0], dtype=jnp.int32)
    spread = (picked[:, None] == tokens[None, :]).astype(jnp.bfloat16)
    rows = jnp.dot(spread, pool, preferred_element_type=jnp.float32).astype(jnp.bfloat16)
    gate = jnp.dot(rows, weights[0], preferred_element_type=jnp.float32) * scale_in
    upper = jnp.dot(rows, weights[1], preferred_element_type=jnp.float32) * scale_in
    sigma = jax.nn.sigmoid(gate)
    active = gate * sigma
    hidden = (active * upper).astype(jnp.bfloat16)
    scaled = (route[:, None] * cotangent.astype(jnp.float32)).astype(jnp.bfloat16)
    back = jnp.dot(scaled, weights[2], preferred_element_type=jnp.float32) * scale_out
    d_gate = (back * upper * sigma * (1.0 + gate * (1.0 - sigma))).astype(jnp.bfloat16)
    d_up = (back * active).astype(jnp.bfloat16)
    grads = jnp.stack(
        [
            (inner(rows, d_gate) * scale_in).astype(jnp.bfloat16),
            (inner(rows, d_up) * scale_in).astype(jnp.bfloat16),
            (inner(scaled, hidden) * scale_out).astype(jnp.bfloat16),
        ]
    )
    sum_gate = inner(spread, d_gate).astype(jnp.bfloat16)
    sum_up = inner(spread, d_up).astype(jnp.bfloat16)
    inputs = (against(sum_gate, weights[0]) + against(sum_up, weights[1])) * scale_in
    return grads, inputs.astype(jnp.bfloat16)


def drain(ref, sem):
    pltpu.make_async_copy(ref, ref, sem).wait()


def exchange(
    narrow_count,
    owners,
    nexts,
    grads,
    master,
    moment_m,
    moment_v,
    master_out,
    m_out,
    v_out,
    next_out,
    recv,
    states,
    part,
    part_in,
    fresh,
    stage,
    loc_sem,
    load_sem,
    save_sem,
    first_send,
    far_recv,
    near_recv,
    part_send,
    part_recv,
    fresh_send,
    fresh_recv,
    out_send,
    out_recv,
    out_loc,
    *fresh_far,
):
    parts, members, block, hidden_units = grads.shape
    half = members // 2
    me = lax.axis_index("wide") * narrow_count + lax.axis_index("narrow")
    group = me // half
    spot = me % half
    base = group * half
    other_base = half - base
    mirror = other_base + spot

    def device(index):
        return (index // narrow_count, index % narrow_count)

    def peer_of(step):
        return (spot + step) % half

    barrier = pltpu.get_barrier_semaphore()

    def greet(step, carry):
        pl.semaphore_signal(
            barrier, inc=1, device_id=device(base + peer_of(step)), device_id_type=MESH
        )
        return carry

    pl.semaphore_signal(barrier, inc=1, device_id=device(mirror), device_id_type=MESH)
    lax.fori_loop(1, half, greet, 0)
    pl.semaphore_wait(barrier, half)

    def send_first(k):
        for start, sem in ((other_base, far_recv), (base, near_recv)):

            def send(step, carry):
                peer = peer_of(step)
                pltpu.make_async_remote_copy(
                    src_ref=grads.at[k, start + peer],
                    dst_ref=recv.at[k, start + spot],
                    send_sem=first_send.at[k],
                    recv_sem=sem.at[k],
                    device_id=device(base + peer),
                    device_id_type=MESH,
                ).start()
                return carry

            lax.fori_loop(1, half, send, 0)

    def own_first(k):
        for start in (other_base, base):
            pltpu.make_async_copy(
                grads.at[k, start + spot], recv.at[k, start + spot], loc_sem.at[k]
            ).start()

    def loads(k):
        for i, ref in enumerate((master, moment_m, moment_v)):
            pltpu.make_async_copy(ref.at[:, k], states.at[i, k], load_sem.at[i, k]).start()

    row_tile = min(ROW_TILE, block)
    col_tile = min(COL_TILE, hidden_units)

    def tiles(body):
        def rows_of(r, carry):
            rows = pl.ds(pl.multiple_of(r * row_tile, row_tile), row_tile)

            def cols_of(c, inside):
                body(rows, pl.ds(pl.multiple_of(c * col_tile, col_tile), col_tile))
                return inside

            return lax.fori_loop(0, hidden_units // col_tile, cols_of, carry)

        lax.fori_loop(0, block // row_tile, rows_of, 0)

    def sums(k, start, rows, cols, init):
        def add(outer, totals):
            for u in range(UNROLL):
                s = outer * UNROLL + u
                value = recv[k, start + s, rows, cols].astype(jnp.float32)
                totals = tuple(
                    total + value * owners[e * members + base + s]
                    for e, total in enumerate(totals)
                )
            return totals

        return lax.fori_loop(0, half // UNROLL, add, init)

    def mirror_copy(src, dst, send, arrive):
        return pltpu.make_async_remote_copy(
            src_ref=src,
            dst_ref=dst,
            send_sem=send,
            recv_sem=arrive,
            device_id=device(mirror),
            device_id_type=MESH,
        )

    def partial(k):
        drain(recv.at[k, pl.ds(0, 2)], loc_sem.at[k])
        drain(recv.at[k, pl.ds(0, half - 1)], far_recv.at[k])

        def body(rows, cols):
            zero = jnp.zeros((row_tile, col_tile), jnp.float32)
            totals = sums(k, other_base, rows, cols, (zero,) * EXPERTS)
            for e, total in enumerate(totals):
                part[k, e, rows, cols] = total.astype(jnp.bfloat16)

        tiles(body)
        mirror_copy(part.at[k], part_in.at[k], part_send.at[k], part_recv.at[k]).start()

    def refill(k, which, owner):
        held = fresh_far[k] if which else fresh.at[k]

        def fill(step, carry):
            peer = peer_of(step)
            stage[k, which * half + peer] = held[nexts[base + peer]]
            pltpu.make_async_remote_copy(
                src_ref=stage.at[k, which * half + peer],
                dst_ref=next_out.at[k, owner],
                send_sem=out_send.at[k],
                recv_sem=out_recv.at[k],
                device_id=device(base + peer),
                device_id_type=MESH,
            ).start()
            return carry

        lax.fori_loop(1, half, fill, 0)
        stage[k, which * half + spot] = held[nexts[base + spot]]
        pltpu.make_async_copy(
            stage.at[k, which * half + spot], next_out.at[k, owner], out_loc.at[k, which]
        ).start()

    def update(k):
        for i in range(3):
            drain(states.at[i, k], load_sem.at[i, k])
        drain(recv.at[k, pl.ds(0, half - 1)], near_recv.at[k])
        drain(part_in.at[k], part_recv.at[k])

        def body(rows, cols):
            init = tuple(
                part_in[k, e, rows, cols].astype(jnp.float32) for e in range(EXPERTS)
            )
            totals = sums(k, base, rows, cols, init)
            for e, grad in enumerate(totals):
                held = states[0, k, e, rows, cols]
                first = 0.9 * states[1, k, e, rows, cols] + 0.1 * grad
                second = 0.95 * states[2, k, e, rows, cols] + 0.05 * grad * grad
                value = held - 0.05 * (first / (jnp.sqrt(second) + 1e-08) + 0.1 * held)
                states[0, k, e, rows, cols] = value
                states[1, k, e, rows, cols] = first
                states[2, k, e, rows, cols] = second
                fresh[k, e, rows, cols] = value.astype(jnp.bfloat16)

        tiles(body)
        mirror_copy(
            fresh.at[k], fresh_far[k], fresh_send.at[k], fresh_recv.at[k]
        ).start()
        refill(k, 0, me)
        for i, ref in enumerate((master_out, m_out, v_out)):
            pltpu.make_async_copy(states.at[i, k], ref.at[:, k], save_sem.at[i, k]).start()

    def relay(k):
        drain(fresh_far[k], fresh_recv.at[k])
        refill(k, 1, mirror)

    ahead = min(2, parts)
    for k in range(ahead):
        send_first(k)
        own_first(k)
    for k in range(parts):
        loads(k)
    for k in range(parts + 2):
        if k < parts:
            partial(k)
            if k + ahead < parts:
                send_first(k + ahead)
                own_first(k + ahead)
        if 1 <= k <= parts:
            update(k - 1)
        if k >= 2:
            relay(k - 2)
    for k in range(parts):
        drain(recv.at[k, pl.ds(0, 2 * (half - 1))], first_send.at[k])
        drain(part.at[k], part_send.at[k])
        drain(fresh.at[k], fresh_send.at[k])
        drain(stage.at[k, pl.ds(0, 2 * (half - 1))], out_send.at[k])
        drain(next_out.at[k, pl.ds(0, 2 * (half - 1))], out_recv.at[k])
        for which in range(2):
            drain(next_out.at[k, which], out_loc.at[k, which])
        for i in range(3):
            drain(states.at[i, k], save_sem.at[i, k])


def local(
    pool_tokens,
    cotangent,
    slot_weights,
    row_index,
    route_weight,
    slot_expert,
    next_expert,
    master,
    moment_m,
    moment_v,
):
    grads, token_grads = slot_pass(
        pool_tokens, row_index[0], cotangent, slot_weights[0], route_weight[0]
    )
    narrow_count = lax.axis_size("narrow")
    members = lax.axis_size("wide") * narrow_count
    parts, width, hidden_units = grads.shape
    block = width // members
    half = members // 2
    owners = (slot_expert[:, 0][None, :] == jnp.arange(EXPERTS, dtype=jnp.int32)[:, None]).astype(
        jnp.float32
    )
    anywhere = pl.BlockSpec(memory_space=pl.ANY)
    scalars = pl.BlockSpec(memory_space=pltpu.SMEM)
    dma = pltpu.SemaphoreType.DMA
    state = jax.ShapeDtypeStruct(master.shape, jnp.float32)
    bf16 = jnp.bfloat16
    fresh, first, second, refilled = pl.pallas_call(
        functools.partial(exchange, narrow_count),
        out_shape=(
            state,
            state,
            state,
            jax.ShapeDtypeStruct((parts, members, block, hidden_units), bf16),
        ),
        in_specs=[scalars, scalars] + [anywhere] * 4,
        out_specs=(anywhere,) * 4,
        scratch_shapes=[
            pltpu.VMEM((parts, members, block, hidden_units), bf16),
            pltpu.VMEM((3, parts, EXPERTS, block, hidden_units), jnp.float32),
            pltpu.VMEM((parts, EXPERTS, block, hidden_units), bf16),
            pltpu.VMEM((parts, EXPERTS, block, hidden_units), bf16),
            pltpu.VMEM((parts, EXPERTS, block, hidden_units), bf16),
            pltpu.VMEM((parts, 2 * half, block, hidden_units), bf16),
            dma((parts,)),
            dma((3, parts)),
            dma((3, parts)),
            dma((parts,)),
            dma((parts,)),
            dma((parts,)),
            dma((parts,)),
            dma((parts,)),
            dma((parts,)),
            dma((parts,)),
            dma((parts,)),
            dma((parts,)),
            dma((parts, 2)),
        ]
        + [pltpu.VMEM((EXPERTS, block, hidden_units), bf16)] * parts,
        compiler_params=pltpu.CompilerParams(
            collective_id=0, has_side_effects=True, vmem_limit_bytes=60 * 1024 * 1024
        ),
    )(
        owners.reshape(-1),
        next_expert[:, 0],
        grads.reshape(parts, members, block, hidden_units),
        master,
        moment_m,
        moment_v,
    )
    next_weights = refilled.reshape(1, parts, width, hidden_units)
    return (token_grads, fresh, first, second, next_weights)


def solution(mesh):
    in_specs = (
        P(("wide", "narrow"), None),
        P(("wide", "narrow"), None),
        P(("wide", "narrow"), None, None, None),
        P(("wide", "narrow"), None),
        P(("wide", "narrow"), None),
        P(),
        P(),
        P(None, None, ("wide", "narrow"), None),
        P(None, None, ("wide", "narrow"), None),
        P(None, None, ("wide", "narrow"), None),
    )
    out_specs = (
        P(("wide", "narrow"), None),
        P(None, None, ("wide", "narrow"), None),
        P(None, None, ("wide", "narrow"), None),
        P(None, None, ("wide", "narrow"), None),
        P(("wide", "narrow"), None, None, None),
    )
    return jax.shard_map(local, mesh=mesh, in_specs=in_specs, out_specs=out_specs, check_vma=False)
```

time: 632 us -> 259 us (0.41); the launches traced: 624 us -> 259 us
  waiting for transfers between devices: 467 us -> 0 us
  Pallas kernels: 0 us -> 215 us
  matrix products: 61.1 us -> 23.4 us
  local copies, waits for them, and re-layouts: 51.1 us -> 14.4 us
  other arithmetic: 31.7 us -> 5.51 us
  starting transfers between devices: 11.2 us -> 0 us
    all_to_all x2 -> x0, waiting for transfers between devices: 467 us -> none  [the longest x1 373 us: local(): lax.all_to_all(grads, ('wide', 'narrow'), split_axis=1, concat_axis=0, ti...]
    pallas_call x0 -> x1, Pallas kernels: none -> 215 us  [local(): pl.pallas_call(functools.partial(exchange, narrow_count), out_shape=(stat...]
    another operation x1 -> x0, local copies, waits for them, and re-layouts: 25.7 us -> none  [slot_pass(): jnp.stack([inner(rows, d_gate) * scale_in, inner(rows, d_up) * scale_in,...]
    dot_general x1, matrix products: 26.7 us -> 1.83 us  [slot_pass(): jnp.dot(spread, pool, preferred_element_type=jnp.float32)]
    scatter-add x1 -> x0, other arithmetic: 18.8 us -> none  [local(): jnp.zeros(pool_tokens.shape, jnp.float32).at[picked].add(inputs)]
    all_to_all x2 -> x0, starting transfers between devices: 11.2 us -> none  [the longest x1 7.45 us: local(): lax.all_to_all(grads, ('wide', 'narrow'), split_axis=1, concat_axis=0, ti...]
    gather x2 -> x0, local copies, waits for them, and re-layouts: 7.89 us -> none  [the longest x1 4.23 us: local(): rows = jnp.take(pool_tokens, picked, axis=0)]
    select_n x3 -> x0, other arithmetic: 6.91 us -> none  [the longest x2 6.09 us: local(): outgoing = jnp.take(reordered, next_expert[:, 0], axis=1)]
  transfers between devices with their start and end apart: 2 -> 0, of which waited for: 2 -> 0; matrix products, arithmetic and copies ran while one was open for 7% -> 0% of each run, Pallas kernels for 0% -> 0%
where the time goes in v1:
time: 259 us
  Pallas kernels  215 us (83%)
  matrix products  23.4 us (9%)
  local copies, waits for them, and re-layouts  14.4 us (6%)
  other arithmetic  5.51 us (2%)
    pallas_call x1, Pallas kernels, local(): pl.pallas_call(functools.partial(exchange, narrow_count), out_shape=(stat...  215 us
    unnamed x18, local copies, waits for them, and re-layouts  13.8 us
    dot_general x2, matrix products, against(): lax.dot_general(left, right, (((1,), (1,)), ((), ())), preferred_element_...  9.9 us
    dot_general x3, matrix products, inner(): lax.dot_general(left, right, (((0,), (0,)), ((), ())), preferred_element_...  5.76 us

profile of v1, /device:TPU:0, one launch (start us, length us, event | category | flops | bytes accessed | tf_op | source)
XLA Modules:
  0.0 258.9 jit_solution(5579516901190316197)
XLA Ops:
  0.6 0.0 copy-start
  0.6 0.8 reduce
  1.5 0.7 reduce.1
  2.2 0.7 fusion.30
  2.8 0.6 reshape.36.owners
  3.5 0.0 copy-done
  3.5 0.0 copy-start.3
  3.5 1.8 convolution_convert_fusion
  5.3 0.9 copy-done.3
  6.3 1.8 fusion.21
  8.0 0.0 copy-start.4
  8.1 1.8 fusion.18
  9.8 0.1 copy-done.4
  9.9 2.3 multiply_convert_fusion.6
  12.3 2.1 multiply_convert_fusion.1
  14.4 1.8 multiply_convert_fusion.2
  16.2 1.8 multiply_convert_fusion.3
  18.1 3.3 %pad_maximum_fusion.grads = bf16[3,32,64,512]{3,2,1,0:T(8,128)(2,1)} fusion(bf16[1,32,64,512]{3,2,1,0:T(8,128)(2,1)S(1)} %bitcast.39, bf16[1,32,64,512]{3,2,1,0:T(8,128)(2,1)S(1)} %bitcast.40, bf16[1,32,64,512]{3,2,1,0:T(8,128)(2,1)S(1)} %bitcast.41), kind=kLoop, calls=%fused_computation | loop fusion | flops 6291456 | bytes 12582912 | tf_op jit(solution)/shard_map/stack | solution.py:44
  21.4 4.7 %fusion = f32[384,2048]{1,0:T(8,128)} fusion(bf16[1,3,2048,512]{3,2,1,0:T(8,128)(2,1)} %param.12, bf16[768,512]{1,0:T(8,128)(2,1)S(1)} %get-tuple-element.14, s32[768]{0:T(1024)S(1)} %reduce), kind=kOutput, calls=%fused_computation.7 | convolution fusion | flops 1107787776 | bytes 6032384 | tf_op jit(solution)/shard_map/dot_general | solution.py:24
  26.2 5.2 %multiply_convert_fusion.4 = bf16[384,2048]{1,0:T(8,128)(2,1)} fusion(f32[384,2048]{1,0:T(8,128)} %fusion, bf16[1,3,2048,512]{3,2,1,0:T(8,128)(2,1)} %param.12, bf16[768,512]{1,0:T(8,128)(2,1)S(1)} %get-tuple-element.13, s32[768]{0:T(1024)S(1)} %reduce), kind=kOutput, calls=%fused_computation.6 | convolution fusion | flops 1110147072 | bytes 7605248 | tf_op jit(solution)/shard_map/dot_general | solution.py:24
  31.3 214.8 %shard_map.137 = (f32[8,3,64,512]{3,2,1,0:T(8,128)}, f32[8,3,64,512]{3,2,1,0:T(8,128)}, f32[8,3,64,512]{3,2,1,0:T(8,128)}, bf16[3,32,64,512]{3,2,1,0:T(8,128)(2,1)}) custom-call(f32[256]{0:T(256)} %reshape.36.owners, s32[32]{0:T(128)} %bitcast.42, bf16[3,32,64,512]{3,2,1,0:T(8,128)(2,1)} %pad_maximum_fusion.grads, f32[8,3,64,512]{3,2,1,0:T(8,128)} %master.1, ...), custom_call_target="tpu_custom_call" | custom-call | tf_op jit(solution)/shard_map/pallas_call | solution.py:310
  246.2 0.0 slice-start
  246.2 4.2 %copy.19 = f32[8,3,64,512]{3,2,1,0:T(8,128)} copy(f32[8,3,64,512]{3,2,1,0:T(8,128)} %get-tuple-element.21) | data formatting | bytes 6291456
  250.4 0.0 copy-start.2
  250.4 0.0 slice-start.1
  250.4 4.2 %copy.20 = f32[8,3,64,512]{3,2,1,0:T(8,128)} copy(f32[8,3,64,512]{3,2,1,0:T(8,128)} %get-tuple-element.22) | data formatting | bytes 6291456
  254.5 0.0 copy-done.2
  254.5 1.7 copy.21
  256.2 0.0 slice-done
  256.2 0.0 slice-done.1
  256.2 0.0 copy-start.1
  256.2 2.7 %copy.22 = bf16[1,3,2048,512]{3,2,1,0:T(8,128)(2,1)} copy(bf16[1,3,2048,512]{3,2,1,0:T(8,128)(2,1)S(1)} %bitcast.38) | data formatting | bytes 12582912
  258.9 0.0 copy-done.1
  (1 shorter events, 0.0 us)
Async XLA Ops:
  0.6 2.8 %copy-start = (bf16[384,2048]{1,0:T(8,128)(2,1)S(1)}, bf16[384,2048]{1,0:T(8,128)(2,1)}, u32[]{:S(2)}) copy-start(bf16[384,2048]{1,0:T(8,128)(2,1)} %param.10) | copy-start | bytes 4718596
  3.5 2.8 %copy-start.3 = (bf16[1,3,2048,512]{3,2,1,0:T(8,128)(2,1)S(1)}, bf16[1,3,2048,512]{3,2,1,0:T(8,128)(2,1)}, u32[]{:S(2)}) copy-start(bf16[1,3,2048,512]{3,2,1,0:T(8,128)(2,1)} %param.12) | copy-start | bytes 18874372
  8.0 1.9 copy-start.4
  246.2 10.0 %slice-start = ((s8[6291456]{0:T(1024)(128)(4,1)}), s8[4194304]{0:T(1024)(128)(4,1)S(1)}, s32[]{:S(2)}) async-start(s8[6291456]{0:T(1024)(128)(4,1)} %bitcast.36), calls=%async_computation | async-start | bytes 8388608
  250.4 4.2 %copy-start.2 = (f32[8,3,64,512]{3,2,1,0:T(8,128)S(1)}, f32[8,3,64,512]{3,2,1,0:T(8,128)}, u32[]{:S(2)}) copy-start(f32[8,3,64,512]{3,2,1,0:T(8,128)} %get-tuple-element.23) | copy-start | bytes 9437188
  250.4 5.8 %slice-start.1 = ((s8[6291456]{0:T(1024)(128)(4,1)}), s8[2097152]{0:T(1024)(128)(4,1)S(1)}, s32[]{:S(2)}) async-start(s8[6291456]{0:T(1024)(128)(4,1)} %bitcast.36), calls=%async_computation.1 | async-start | bytes 4194304
  256.2 2.7 %copy-start.1 = (bf16[384,2048]{1,0:T(8,128)(2,1)S(1)}, bf16[384,2048]{1,0:T(8,128)(2,1)}, u32[]{:S(2)}) copy-start(bf16[384,2048]{1,0:T(8,128)(2,1)} %param.10) | copy-start | bytes 4718596

commit v2 on v1

--- a/solution.py
+++ b/solution.py
@@ -11,6 +11,7 @@
 MESH = pl.DeviceIdType.MESH
 ROW_TILE = 16
 COL_TILE = 256
+WIDE_TILE = 256
 UNROLL = 4
 
 
@@ -26,32 +27,23 @@
     )
 
 
-def slot_pass(pool, picked, cotangent, weights, route):
+def slot_pass(pool, row_index, cotangent, weights, route):
     scale_in = weights.shape[1] ** (-0.5)
     scale_out = weights.shape[2] ** (-0.5)
     tokens = jnp.arange(pool.shape[0], dtype=jnp.int32)
-    spread = (picked[:, None] == tokens[None, :]).astype(jnp.bfloat16)
-    rows = jnp.dot(spread, pool, preferred_element_type=jnp.float32).astype(jnp.bfloat16)
+    spread = (tokens[:, None] == row_index).astype(jnp.bfloat16)
+    rows = inner(spread, pool).astype(jnp.bfloat16)
     gate = jnp.dot(rows, weights[0], preferred_element_type=jnp.float32) * scale_in
     upper = jnp.dot(rows, weights[1], preferred_element_type=jnp.float32) * scale_in
     sigma = jax.nn.sigmoid(gate)
     active = gate * sigma
     hidden = (active * upper).astype(jnp.bfloat16)
-    scaled = (route[:, None] * cotangent.astype(jnp.float32)).astype(jnp.bfloat16)
+    scaled = (route.T * cotangent.astype(jnp.float32)).astype(jnp.bfloat16)
     back = jnp.dot(scaled, weights[2], preferred_element_type=jnp.float32) * scale_out
     d_gate = (back * upper * sigma * (1.0 + gate * (1.0 - sigma))).astype(jnp.bfloat16)
     d_up = (back * active).astype(jnp.bfloat16)
-    grads = jnp.stack(
-        [
-            (inner(rows, d_gate) * scale_in).astype(jnp.bfloat16),
-            (inner(rows, d_up) * scale_in).astype(jnp.bfloat16),
-            (inner(scaled, hidden) * scale_out).astype(jnp.bfloat16),
-        ]
-    )
-    sum_gate = inner(spread, d_gate).astype(jnp.bfloat16)
-    sum_up = inner(spread, d_up).astype(jnp.bfloat16)
-    inputs = (against(sum_gate, weights[0]) + against(sum_up, weights[1])) * scale_in
-    return grads, inputs.astype(jnp.bfloat16)
+    down_grad = (inner(scaled, hidden) * scale_out).astype(jnp.bfloat16)
+    return rows, d_gate, d_up, down_grad
 
 
 def drain(ref, sem):
@@ -60,9 +52,15 @@
 
 def exchange(
     narrow_count,
-    owners,
+    members,
+    experts_now,
     nexts,
-    grads,
+    row_index,
+    down_grad,
+    rows_in,
+    d_gate_in,
+    d_up_in,
+    weights,
     master,
     moment_m,
     moment_v,
@@ -70,15 +68,21 @@
     m_out,
     v_out,
     next_out,
+    tokens_out,
+    owners,
+    made,
+    rows_held,
+    d_held,
+    w_held,
+    token_sums,
     recv,
-    states,
     part,
     part_in,
     fresh,
     stage,
+    in_sem,
     loc_sem,
     load_sem,
-    save_sem,
     first_send,
     far_recv,
     near_recv,
@@ -91,7 +95,10 @@
     out_loc,
     *fresh_far,
 ):
-    parts, members, block, hidden_units = grads.shape
+    parts, _, block, hidden_units = recv.shape
+    width = made.shape[1]
+    scale_in = width ** (-0.5)
+    states = (master_out, m_out, v_out)
     half = members // 2
     me = lax.axis_index("wide") * narrow_count + lax.axis_index("narrow")
     group = me // half
@@ -118,13 +125,54 @@
     lax.fori_loop(1, half, greet, 0)
     pl.semaphore_wait(barrier, half)
 
+    def source(k, owner):
+        span = pl.ds(pl.multiple_of(owner * block, block), block)
+        return down_grad.at[span] if k == parts - 1 else made.at[k, span]
+
+    def wide_tiles(body):
+        tile = min(WIDE_TILE, width)
+
+        def step(t, carry):
+            body(pl.ds(pl.multiple_of(t * tile, tile), tile))
+            return carry
+
+        lax.fori_loop(0, width // tile, step, 0)
+
+    def make(k):
+        def body(span):
+            product = inner(rows_held[:, span], d_held[k])
+            made[k, span, :] = (product * scale_in).astype(jnp.bfloat16)
+
+        wide_tiles(body)
+
+    def token_grads():
+        shape = (token_sums.shape[1], row_index.shape[1])
+        tokens = lax.broadcasted_iota(jnp.int32, shape, 0)
+        spread = jnp.where(tokens == row_index[...], 1.0, 0.0).astype(jnp.bfloat16)
+        for k in range(parts - 1):
+            token_sums[k] = jnp.dot(
+                spread, d_held[k], preferred_element_type=jnp.float32
+            ).astype(jnp.bfloat16)
+
+        def body(span):
+            total = against(token_sums[0], w_held[0, span, :])
+            total = total + against(token_sums[1], w_held[1, span, :])
+            tokens_out[:, span] = (total * scale_in).astype(jnp.bfloat16)
+
+        wide_tiles(body)
+
+    def tabulate(slot, carry):
+        for e in range(EXPERTS):
+            owners[e * members + slot] = jnp.where(experts_now[slot] == e, 1.0, 0.0)
+        return carry
+
     def send_first(k):
         for start, sem in ((other_base, far_recv), (base, near_recv)):
 
             def send(step, carry):
                 peer = peer_of(step)
                 pltpu.make_async_remote_copy(
-                    src_ref=grads.at[k, start + peer],
+                    src_ref=source(k, start + peer),
                     dst_ref=recv.at[k, start + spot],
                     send_sem=first_send.at[k],
                     recv_sem=sem.at[k],
@@ -138,12 +186,12 @@
     def own_first(k):
         for start in (other_base, base):
             pltpu.make_async_copy(
-                grads.at[k, start + spot], recv.at[k, start + spot], loc_sem.at[k]
+                source(k, start + spot), recv.at[k, start + spot], loc_sem.at[k]
             ).start()
 
     def loads(k):
         for i, ref in enumerate((master, moment_m, moment_v)):
-            pltpu.make_async_copy(ref.at[:, k], states.at[i, k], load_sem.at[i, k]).start()
+            pltpu.make_async_copy(ref.at[:, k], states[i].at[:, k], load_sem.at[i, k]).start()
 
     row_tile = min(ROW_TILE, block)
     col_tile = min(COL_TILE, hidden_units)
@@ -220,7 +268,7 @@
 
     def update(k):
         for i in range(3):
-            drain(states.at[i, k], load_sem.at[i, k])
+            drain(states[i].at[:, k], load_sem.at[i, k])
         drain(recv.at[k, pl.ds(0, half - 1)], near_recv.at[k])
         drain(part_in.at[k], part_recv.at[k])
 
@@ -230,13 +278,13 @@
             )
             totals = sums(k, base, rows, cols, init)
             for e, grad in enumerate(totals):
-                held = states[0, k, e, rows, cols]
-                first = 0.9 * states[1, k, e, rows, cols] + 0.1 * grad
-                second = 0.95 * states[2, k, e, rows, cols] + 0.05 * grad * grad
+                held = states[0][e, k, rows, cols]
+                first = 0.9 * states[1][e, k, rows, cols] + 0.1 * grad
+                second = 0.95 * states[2][e, k, rows, cols] + 0.05 * grad * grad
                 value = held - 0.05 * (first / (jnp.sqrt(second) + 1e-08) + 0.1 * held)
-                states[0, k, e, rows, cols] = value
-                states[1, k, e, rows, cols] = first
-                states[2, k, e, rows, cols] = second
+                states[0][e, k, rows, cols] = value
+                states[1][e, k, rows, cols] = first
+                states[2][e, k, rows, cols] = second
                 fresh[k, e, rows, cols] = value.astype(jnp.bfloat16)
 
         tiles(body)
@@ -244,29 +292,43 @@
             fresh.at[k], fresh_far[k], fresh_send.at[k], fresh_recv.at[k]
         ).start()
         refill(k, 0, me)
-        for i, ref in enumerate((master_out, m_out, v_out)):
-            pltpu.make_async_copy(states.at[i, k], ref.at[:, k], save_sem.at[i, k]).start()
 
     def relay(k):
         drain(fresh_far[k], fresh_recv.at[k])
         refill(k, 1, mirror)
 
-    ahead = min(2, parts)
-    for k in range(ahead):
-        send_first(k)
-        own_first(k)
-    for k in range(parts):
+    order = (parts - 1,) + tuple(range(parts - 1))
+    send_first(order[0])
+    own_first(order[0])
+    inputs = (
+        (rows_in, rows_held),
+        (d_gate_in, d_held.at[0]),
+        (d_up_in, d_held.at[1]),
+        (weights.at[0, pl.ds(0, 2)], w_held),
+    )
+    for i, (src, dst) in enumerate(inputs):
+        pltpu.make_async_copy(src, dst, in_sem.at[i]).start()
+    for k in order:
         loads(k)
-    for k in range(parts + 2):
-        if k < parts:
-            partial(k)
-            if k + ahead < parts:
-                send_first(k + ahead)
-                own_first(k + ahead)
-        if 1 <= k <= parts:
-            update(k - 1)
-        if k >= 2:
-            relay(k - 2)
+    for i, (src, dst) in enumerate(inputs):
+        pltpu.make_async_copy(src, dst, in_sem.at[i]).wait()
+    make(order[1])
+    send_first(order[1])
+    own_first(order[1])
+    for k in order[2:]:
+        make(k)
+    lax.fori_loop(0, members, tabulate, 0)
+    token_grads()
+    for step in range(parts + 2):
+        if step < parts:
+            partial(order[step])
+            if step + 2 < parts:
+                send_first(order[step + 2])
+                own_first(order[step + 2])
+        if 1 <= step <= parts:
+            update(order[step - 1])
+        if step >= 2:
+            relay(order[step - 2])
     for k in range(parts):
         drain(recv.at[k, pl.ds(0, 2 * (half - 1))], first_send.at[k])
         drain(part.at[k], part_send.at[k])
@@ -275,8 +337,6 @@
         drain(next_out.at[k, pl.ds(0, 2 * (half - 1))], out_recv.at[k])
         for which in range(2):
             drain(next_out.at[k, which], out_loc.at[k, which])
-        for i in range(3):
-            drain(states.at[i, k], save_sem.at[i, k])
 
 
 def local(
@@ -291,41 +351,45 @@
     moment_m,
     moment_v,
 ):
-    grads, token_grads = slot_pass(
-        pool_tokens, row_index[0], cotangent, slot_weights[0], route_weight[0]
+    rows, d_gate, d_up, down_grad = slot_pass(
+        pool_tokens, row_index, cotangent, slot_weights[0], route_weight
     )
     narrow_count = lax.axis_size("narrow")
     members = lax.axis_size("wide") * narrow_count
-    parts, width, hidden_units = grads.shape
+    parts, width, hidden_units = slot_weights.shape[1:]
     block = width // members
     half = members // 2
-    owners = (slot_expert[:, 0][None, :] == jnp.arange(EXPERTS, dtype=jnp.int32)[:, None]).astype(
-        jnp.float32
-    )
     anywhere = pl.BlockSpec(memory_space=pl.ANY)
     scalars = pl.BlockSpec(memory_space=pltpu.SMEM)
     dma = pltpu.SemaphoreType.DMA
-    state = jax.ShapeDtypeStruct(master.shape, jnp.float32)
     bf16 = jnp.bfloat16
-    fresh, first, second, refilled = pl.pallas_call(
-        functools.partial(exchange, narrow_count),
+    state = pltpu.VMEM(master.shape, jnp.float32)
+    held = pl.BlockSpec(memory_space=pltpu.VMEM)
+    fresh, first, second, refilled, token_grads = pl.pallas_call(
+        functools.partial(exchange, narrow_count, members),
         out_shape=(
             state,
             state,
             state,
-            jax.ShapeDtypeStruct((parts, members, block, hidden_units), bf16),
+            pltpu.VMEM((parts, members, block, hidden_units), bf16),
+            pltpu.VMEM(pool_tokens.shape, bf16),
         ),
-        in_specs=[scalars, scalars] + [anywhere] * 4,
-        out_specs=(anywhere,) * 4,
+        in_specs=[scalars, scalars, held] + [anywhere] * 8,
+        out_specs=(held,) * 5,
         scratch_shapes=[
+            pltpu.SMEM((EXPERTS * members,), jnp.float32),
+            pltpu.VMEM((parts - 1, width, hidden_units), bf16),
+            pltpu.VMEM(rows.shape, bf16),
+            pltpu.VMEM((2,) + d_gate.shape, bf16),
+            pltpu.VMEM((2, width, hidden_units), bf16),
+            pltpu.VMEM((2, pool_tokens.shape[0], hidden_units), bf16),
             pltpu.VMEM((parts, members, block, hidden_units), bf16),
-            pltpu.VMEM((3, parts, EXPERTS, block, hidden_units), jnp.float32),
             pltpu.VMEM((parts, EXPERTS, block, hidden_units), bf16),
             pltpu.VMEM((parts, EXPERTS, block, hidden_units), bf16),
             pltpu.VMEM((parts, EXPERTS, block, hidden_units), bf16),
             pltpu.VMEM((parts, 2 * half, block, hidden_units), bf16),
-            dma((parts,)),
-            dma((3, parts)),
+            dma((4,)),
+            dma((parts,)),
             dma((3, parts)),
             dma((parts,)),
             dma((parts,)),
@@ -340,12 +404,17 @@
         ]
         + [pltpu.VMEM((EXPERTS, block, hidden_units), bf16)] * parts,
         compiler_params=pltpu.CompilerParams(
-            collective_id=0, has_side_effects=True, vmem_limit_bytes=60 * 1024 * 1024
+            collective_id=0, has_side_effects=True, vmem_limit_bytes=42 * 1024 * 1024
         ),
     )(
-        owners.reshape(-1),
+        slot_expert[:, 0],
         next_expert[:, 0],
-        grads.reshape(parts, members, block, hidden_units),
+        row_index,
+        down_grad,
+        rows,
+        d_gate,
+        d_up,
+        slot_weights,
         master,
         moment_m,
         moment_v,

time: 259 us -> 240 us (0.927)
  matrix products: 23.4 us -> 12.3 us
  local copies, waits for them, and re-layouts: 14.4 us -> 9.88 us
  other arithmetic: 5.51 us -> 1.52 us
    dot_general x3 -> x0, matrix products: 11.7 us -> none  [the longest x2 9.9 us: against(): lax.dot_general(left, right, (((1,), (1,)), ((), ())), preferred_element_...]
    unnamed x18 -> x13, local copies, waits for them, and re-layouts: 13.8 us -> 9.88 us
    another operation x1 -> x0, other arithmetic: 3.33 us -> none  [slot_pass(): jnp.stack([(inner(rows, d_gate) * scale_in).astype(jnp.bfloat16), (inner(...]
    dot_general x3 -> x2, matrix products: 5.76 us -> 5.25 us  [inner(): lax.dot_general(left, right, (((0,), (0,)), ((), ())), preferred_element_...]
where the time goes in v2:
time: 240 us; the launch traced here: 239 us
  Pallas kernels  215 us (90%)
  matrix products  12.3 us (5%)
  local copies, waits for them, and re-layouts  9.88 us (4%)
    pallas_call x1, Pallas kernels, local(): pl.pallas_call(functools.partial(exchange, narrow_count, members), out_sh...  215 us
    unnamed x13, local copies, waits for them, and re-layouts  9.88 us
    dot_general x2, matrix products, inner(): lax.dot_general(left, right, (((0,), (0,)), ((), ())), preferred_element_...  5.25 us

profile of v2, /device:TPU:0, one launch (start us, length us, event | category | flops | bytes accessed | tf_op | source)
XLA Modules:
  0.0 239.3 jit_solution(7468761649566266798)
XLA Ops:
  0.6 0.0 copy-start
  0.6 0.8 reduce
  1.5 0.7 reduce.1
  2.2 0.0 copy-done
  2.2 0.0 copy-start.1
  2.2 1.8 convolution_convert_fusion.rows_in
  4.0 0.9 copy-done.1
  5.0 0.0 copy-start.2
  5.0 1.8 fusion.13
  6.8 0.0 copy-done.2
  6.8 0.0 copy-start.3
  6.8 1.8 fusion.10
  8.6 0.1 copy-done.3
  8.7 3.5 %multiply_convert_fusion.2 = (bf16[768,512]{1,0:T(8,128)(2,1)}, bf16[768,512]{1,0:T(8,128)(2,1)}) fusion(f32[768,512]{1,0:T(8,128)S(1)} %fusion.10, f32[768,512]{1,0:T(8,128)S(1)} %fusion.13, bf16[1,3,2048,512]{3,2,1,0:T(8,128)(2,1)S(1)} %copy-done.1, bf16[768,2048]{1,0:T(8,128)(2,1)S(1)} %copy-done.3, f32[768]{0:T(1024)S(1)} %reduce), kind=kOutput, calls=%fused_computation.12 | convolution fusion | flops 1620836352 | bytes 9965568 | tf_op jit(solution)/shard_map/dot_general | solution.py:42
  12.1 3.4 %multiply_convert_fusion.1.down_grad = bf16[2048,512]{1,0:T(8,128)(2,1)} fusion(bf16[768,2048]{1,0:T(8,128)(2,1)S(1)} %copy-done.3, f32[768]{0:T(1024)S(1)} %reduce, f32[768,512]{1,0:T(8,128)S(1)} %fusion.13, f32[768,512]{1,0:T(8,128)S(1)} %fusion.10), kind=kOutput, calls=%fused_computation.1 | convolution fusion | flops 1619787776 | bytes 8391680 | tf_op jit(solution)/shard_map/dot_general | solution.py:19
  15.5 214.9 %shard_map.137 = (f32[8,3,64,512]{3,2,1,0:T(8,128)S(1)}, f32[8,3,64,512]{3,2,1,0:T(8,128)S(1)}, f32[8,3,64,512]{3,2,1,0:T(8,128)S(1)}, bf16[3,32,64,512]{3,2,1,0:T(8,128)(2,1)S(1)}, bf16[384,2048]{1,0:T(8,128)(2,1)S(1)}) custom-call(s32[32]{0:T(128)} %bitcast.24, s32[32]{0:T(128)} %bitcast.25, s32[1,768]{1,0:T(1,128)} %row_index.1, ...), custom_call_target="tpu_custom_call" | custom-call | tf_op jit(solution)/shard_map/pallas_call | solution.py:368
  230.4 1.1 copy.20
  231.6 1.7 copy.21
  233.2 1.7 copy.22
  234.9 1.7 copy.23
  236.6 2.7 %copy.24 = bf16[1,3,2048,512]{3,2,1,0:T(8,128)(2,1)} copy(bf16[1,3,2048,512]{3,2,1,0:T(8,128)(2,1)S(1)} %bitcast.23) | data formatting | bytes 12582912
Async XLA Ops:
  0.6 1.5 copy-start
  2.2 2.8 %copy-start.1 = (bf16[1,3,2048,512]{3,2,1,0:T(8,128)(2,1)S(1)}, bf16[1,3,2048,512]{3,2,1,0:T(8,128)(2,1)}, u32[]{:S(2)}) copy-start(bf16[1,3,2048,512]{3,2,1,0:T(8,128)(2,1)} %weights.1) | copy-start | bytes 18874372
  5.0 1.8 copy-start.2
  6.8 1.9 copy-start.3

commit v3 on v2

--- a/solution.py
+++ b/solution.py
@@ -12,6 +12,7 @@
 ROW_TILE = 16
 COL_TILE = 256
 WIDE_TILE = 256
+LONG_TILE = 256
 UNROLL = 4
 
 
@@ -25,25 +26,6 @@
     return lax.dot_general(
         left, right, (((1,), (1,)), ((), ())), preferred_element_type=jnp.float32
     )
-
-
-def slot_pass(pool, row_index, cotangent, weights, route):
-    scale_in = weights.shape[1] ** (-0.5)
-    scale_out = weights.shape[2] ** (-0.5)
-    tokens = jnp.arange(pool.shape[0], dtype=jnp.int32)
-    spread = (tokens[:, None] == row_index).astype(jnp.bfloat16)
-    rows = inner(spread, pool).astype(jnp.bfloat16)
-    gate = jnp.dot(rows, weights[0], preferred_element_type=jnp.float32) * scale_in
-    upper = jnp.dot(rows, weights[1], preferred_element_type=jnp.float32) * scale_in
-    sigma = jax.nn.sigmoid(gate)
-    active = gate * sigma
-    hidden = (active * upper).astype(jnp.bfloat16)
-    scaled = (route.T * cotangent.astype(jnp.float32)).astype(jnp.bfloat16)
-    back = jnp.dot(scaled, weights[2], preferred_element_type=jnp.float32) * scale_out
-    d_gate = (back * upper * sigma * (1.0 + gate * (1.0 - sigma))).astype(jnp.bfloat16)
-    d_up = (back * active).astype(jnp.bfloat16)
-    down_grad = (inner(scaled, hidden) * scale_out).astype(jnp.bfloat16)
-    return rows, d_gate, d_up, down_grad
 
 
 def drain(ref, sem):
@@ -56,10 +38,9 @@
     experts_now,
     nexts,
     row_index,
-    down_grad,
-    rows_in,
-    d_gate_in,
-    d_up_in,
+    route,
+    pool,
+    cotangent,
     weights,
     master,
     moment_m,
@@ -72,6 +53,11 @@
     owners,
     made,
     rows_held,
+    cot_held,
+    spread,
+    route_column,
+    gates,
+    hidden,
     d_held,
     w_held,
     token_sums,
@@ -79,7 +65,6 @@
     part,
     part_in,
     fresh,
-    stage,
     in_sem,
     loc_sem,
     load_sem,
@@ -98,6 +83,7 @@
     parts, _, block, hidden_units = recv.shape
     width = made.shape[1]
     scale_in = width ** (-0.5)
+    scale_out = hidden_units ** (-0.5)
     states = (master_out, m_out, v_out)
     half = members // 2
     me = lax.axis_index("wide") * narrow_count + lax.axis_index("narrow")
@@ -123,11 +109,9 @@
 
     pl.semaphore_signal(barrier, inc=1, device_id=device(mirror), device_id_type=MESH)
     lax.fori_loop(1, half, greet, 0)
-    pl.semaphore_wait(barrier, half)
-
     def source(k, owner):
         span = pl.ds(pl.multiple_of(owner * block, block), block)
-        return down_grad.at[span] if k == parts - 1 else made.at[k, span]
+        return made.at[k, span]
 
     def wide_tiles(body):
         tile = min(WIDE_TILE, width)
@@ -140,18 +124,61 @@
 
     def make(k):
         def body(span):
-            product = inner(rows_held[:, span], d_held[k])
-            made[k, span, :] = (product * scale_in).astype(jnp.bfloat16)
+            if k == parts - 1:
+                product = inner(cot_held[:, span], hidden[...]) * scale_out
+            else:
+                product = inner(rows_held[:, span], d_held[k]) * scale_in
+            made[k, span, :] = product.astype(jnp.bfloat16)
 
         wide_tiles(body)
 
+    def long_tiles(body):
+        length = rows_held.shape[0]
+        tile = min(LONG_TILE, length)
+
+        def step(t, carry):
+            body(pl.ds(pl.multiple_of(t * tile, tile), tile))
+            return carry
+
+        lax.fori_loop(0, length // tile, step, 0)
+
+    def product_of(left, right):
+        return jnp.dot(left, right, preferred_element_type=jnp.float32)
+
+    def pick_rows():
+        tokens = lax.broadcasted_iota(jnp.int32, spread.shape, 0)
+        spread[...] = jnp.where(tokens == row_index[...], 1.0, 0.0).astype(jnp.bfloat16)
+        length = rows_held.shape[0]
+        route_column[...] = jnp.transpose(jnp.broadcast_to(route[...], (128, length)))
+
+    def gather(span):
+        rows_held[:, span] = inner(spread[...], tokens_out[:, span]).astype(jnp.bfloat16)
+
+    def forward(span):
+        rows = rows_held[span, :]
+        gate = product_of(rows, w_held[0]) * scale_in
+        upper = product_of(rows, w_held[1]) * scale_in
+        gates[0, span, :] = gate
+        gates[1, span, :] = upper
+        hidden[span, :] = (gate * jax.nn.sigmoid(gate) * upper).astype(jnp.bfloat16)
+
+    def scale_rows(span):
+        column = route_column[span, pl.ds(0, 1)]
+        cot_held[span, :] = (column * cot_held[span, :].astype(jnp.float32)).astype(jnp.bfloat16)
+
+    def backward(span):
+        back = product_of(cot_held[span, :], w_held[2]) * scale_out
+        gate = gates[0, span, :]
+        upper = gates[1, span, :]
+        sigma = jax.nn.sigmoid(gate)
+        slope = sigma * (1.0 + gate * (1.0 - sigma))
+        d_held[0, span, :] = (back * upper * slope).astype(jnp.bfloat16)
+        d_held[1, span, :] = (back * (gate * sigma)).astype(jnp.bfloat16)
+
     def token_grads():
-        shape = (token_sums.shape[1], row_index.shape[1])
-        tokens = lax.broadcasted_iota(jnp.int32, shape, 0)
-        spread = jnp.where(tokens == row_index[...], 1.0, 0.0).astype(jnp.bfloat16)
         for k in range(parts - 1):
             token_sums[k] = jnp.dot(
-                spread, d_held[k], preferred_element_type=jnp.float32
+                spread[...], d_held[k], preferred_element_type=jnp.float32
             ).astype(jnp.bfloat16)
 
         def body(span):
@@ -249,9 +276,9 @@
 
         def fill(step, carry):
             peer = peer_of(step)
-            stage[k, which * half + peer] = held[nexts[base + peer]]
+            recv[k, which * half + peer] = held[nexts[base + peer]]
             pltpu.make_async_remote_copy(
-                src_ref=stage.at[k, which * half + peer],
+                src_ref=recv.at[k, which * half + peer],
                 dst_ref=next_out.at[k, owner],
                 send_sem=out_send.at[k],
                 recv_sem=out_recv.at[k],
@@ -261,9 +288,9 @@
             return carry
 
         lax.fori_loop(1, half, fill, 0)
-        stage[k, which * half + spot] = held[nexts[base + spot]]
+        recv[k, which * half + spot] = held[nexts[base + spot]]
         pltpu.make_async_copy(
-            stage.at[k, which * half + spot], next_out.at[k, owner], out_loc.at[k, which]
+            recv.at[k, which * half + spot], next_out.at[k, owner], out_loc.at[k, which]
         ).start()
 
     def update(k):
@@ -298,20 +325,26 @@
         refill(k, 1, mirror)
 
     order = (parts - 1,) + tuple(range(parts - 1))
+    inputs = ((pool, tokens_out), (weights.at[0], w_held), (cotangent, cot_held))
+    arrivals = [
+        pltpu.make_async_copy(src, dst, in_sem.at[i]) for i, (src, dst) in enumerate(inputs)
+    ]
+    for arrival in arrivals:
+        arrival.start()
+    pick_rows()
+    arrivals[0].wait()
+    wide_tiles(gather)
+    arrivals[1].wait()
+    long_tiles(forward)
+    arrivals[2].wait()
+    long_tiles(scale_rows)
+    make(order[0])
+    pl.semaphore_wait(barrier, half)
     send_first(order[0])
     own_first(order[0])
-    inputs = (
-        (rows_in, rows_held),
-        (d_gate_in, d_held.at[0]),
-        (d_up_in, d_held.at[1]),
-        (weights.at[0, pl.ds(0, 2)], w_held),
-    )
-    for i, (src, dst) in enumerate(inputs):
-        pltpu.make_async_copy(src, dst, in_sem.at[i]).start()
     for k in order:
         loads(k)
-    for i, (src, dst) in enumerate(inputs):
-        pltpu.make_async_copy(src, dst, in_sem.at[i]).wait()
+    long_tiles(backward)
     make(order[1])
     send_first(order[1])
     own_first(order[1])
@@ -333,7 +366,7 @@
         drain(recv.at[k, pl.ds(0, 2 * (half - 1))], first_send.at[k])
         drain(part.at[k], part_send.at[k])
         drain(fresh.at[k], fresh_send.at[k])
-        drain(stage.at[k, pl.ds(0, 2 * (half - 1))], out_send.at[k])
+        drain(recv.at[k, pl.ds(0, 2 * (half - 1))], out_send.at[k])
         drain(next_out.at[k, pl.ds(0, 2 * (half - 1))], out_recv.at[k])
         for which in range(2):
             drain(next_out.at[k, which], out_loc.at[k, which])
@@ -351,14 +384,12 @@
     moment_m,
     moment_v,
 ):
-    rows, d_gate, d_up, down_grad = slot_pass(
-        pool_tokens, row_index, cotangent, slot_weights[0], route_weight
-    )
     narrow_count = lax.axis_size("narrow")
     members = lax.axis_size("wide") * narrow_count
     parts, width, hidden_units = slot_weights.shape[1:]
     block = width // members
-    half = members // 2
+    length = row_index.shape[1]
+    pool_count = pool_tokens.shape[0]
     anywhere = pl.BlockSpec(memory_space=pl.ANY)
     scalars = pl.BlockSpec(memory_space=pltpu.SMEM)
     dma = pltpu.SemaphoreType.DMA
@@ -374,21 +405,25 @@
             pltpu.VMEM((parts, members, block, hidden_units), bf16),
             pltpu.VMEM(pool_tokens.shape, bf16),
         ),
-        in_specs=[scalars, scalars, held] + [anywhere] * 8,
+        in_specs=[scalars, scalars, held, held] + [anywhere] * 6,
         out_specs=(held,) * 5,
         scratch_shapes=[
             pltpu.SMEM((EXPERTS * members,), jnp.float32),
-            pltpu.VMEM((parts - 1, width, hidden_units), bf16),
-            pltpu.VMEM(rows.shape, bf16),
-            pltpu.VMEM((2,) + d_gate.shape, bf16),
-            pltpu.VMEM((2, width, hidden_units), bf16),
-            pltpu.VMEM((2, pool_tokens.shape[0], hidden_units), bf16),
+            pltpu.VMEM((parts, width, hidden_units), bf16),
+            pltpu.VMEM((length, width), bf16),
+            pltpu.VMEM((length, width), bf16),
+            pltpu.VMEM((pool_count, length), bf16),
+            pltpu.VMEM((length, 128), jnp.float32),
+            pltpu.VMEM((2, length, hidden_units), jnp.float32),
+            pltpu.VMEM((length, hidden_units), bf16),
+            pltpu.VMEM((2, length, hidden_units), bf16),
+            pltpu.VMEM((parts, width, hidden_units), bf16),
+            pltpu.VMEM((2, pool_count, hidden_units), bf16),
             pltpu.VMEM((parts, members, block, hidden_units), bf16),
             pltpu.VMEM((parts, EXPERTS, block, hidden_units), bf16),
             pltpu.VMEM((parts, EXPERTS, block, hidden_units), bf16),
             pltpu.VMEM((parts, EXPERTS, block, hidden_units), bf16),
-            pltpu.VMEM((parts, 2 * half, block, hidden_units), bf16),
-            dma((4,)),
+            dma((3,)),
             dma((parts,)),
             dma((3, parts)),
             dma((parts,)),
@@ -404,16 +439,15 @@
         ]
         + [pltpu.VMEM((EXPERTS, block, hidden_units), bf16)] * parts,
         compiler_params=pltpu.CompilerParams(
-            collective_id=0, has_side_effects=True, vmem_limit_bytes=42 * 1024 * 1024
+            collective_id=0, has_side_effects=True, vmem_limit_bytes=46 * 1024 * 1024
         ),
     )(
         slot_expert[:, 0],
         next_expert[:, 0],
         row_index,
-        down_grad,
-        rows,
-        d_gate,
-        d_up,
+        route_weight,
+        pool_tokens,
+        cotangent,
         slot_weights,
         master,
         moment_m,

time: 240 us -> 235 us (0.979)
  matrix products: 12.3 us -> 0 us
  Pallas kernels: 215 us -> 226 us
    dot_general x5 -> x0, matrix products: 12.3 us -> none  [the longest x2 5.25 us: inner(): lax.dot_general(left, right, (((0,), (0,)), ((), ())), preferred_element_...]
    pallas_call x1, Pallas kernels: 215 us -> 226 us  [local(): pl.pallas_call(functools.partial(exchange, narrow_count, members), out_sh...]
    unnamed x13 -> x5, local copies, waits for them, and re-layouts: 9.88 us -> 8.84 us
where the time goes in v3:
time: 235 us
  Pallas kernels  226 us (96%)
  local copies, waits for them, and re-layouts  8.84 us (4%)
    pallas_call x1, Pallas kernels, local(): pl.pallas_call(functools.partial(exchange, narrow_count, members), out_sh...  226 us
    unnamed x5, local copies, waits for them, and re-layouts  8.84 us

profile of v3, /device:TPU:0, one launch (start us, length us, event | category | flops | bytes accessed | tf_op | source)
XLA Modules:
  0.0 235.1 jit_solution(1662820952572176766)
XLA Ops:
  0.6 225.6 %shard_map.137 = (f32[8,3,64,512]{3,2,1,0:T(8,128)S(1)}, f32[8,3,64,512]{3,2,1,0:T(8,128)S(1)}, f32[8,3,64,512]{3,2,1,0:T(8,128)S(1)}, bf16[3,32,64,512]{3,2,1,0:T(8,128)(2,1)S(1)}, bf16[384,2048]{1,0:T(8,128)(2,1)S(1)}) custom-call(s32[32]{0:T(128)} %bitcast.4, s32[32]{0:T(128)} %bitcast.5, s32[1,768]{1,0:T(1,128)} %row_index.1, f32[1,768]{1,0:T(1,128)} %route.1, ...), custom_call_target="tpu_custom_call" | custom-call | tf_op jit(solution)/shard_map/pallas_call | solution.py:399
  226.3 1.1 copy.20
  227.4 1.7 copy.21
  229.1 1.7 copy.22
  230.8 1.7 copy.23
  232.4 2.7 %copy.24 = bf16[1,3,2048,512]{3,2,1,0:T(8,128)(2,1)} copy(bf16[1,3,2048,512]{3,2,1,0:T(8,128)(2,1)S(1)} %bitcast.3) | data formatting | bytes 12582912
